TPU v7x, 256 devices: a whole 4x4x8 slice. The times are simulated.
256 devices in a mesh: sec: 2 (over y_hi), row: 64 (over z, x, y_lo), col: 2 (over core).
Axes of the slice: x: 4, y: 4 (y_hi: 2, y_lo: 2; y = y_hi * 2 + y_lo), z: 8, core: 2. Of those that a mesh axis runs over, the one named last changes fastest.
Arguments:
- basis_matrix: bfloat16 [81920, 4096], P('row', 'col'), may hold values from -6 to 6
- operator_blocks: bfloat16 [640, 7, 128, 128], P('row', None, 'sec'), may hold values from -0.1875 to 0.1875
- neighbours: int32 [640, 7], P('row'), may hold values from 0 to 639, as said below
- neighbour_mask: int32 [640, 7], P('row'), may hold values from 0 to 1, as said below
Outputs:
- reduced: float32 [4096, 4096], P(('sec', 'row'), 'col')
Inputs may be any that keep to these rules, and one draw needn't show every extreme that they name: `neighbours`: slot 0 of row block b is b; slots 1 to 4 are b - 1, b + 1, b - 2, b + 2; slots 5 and 6 lie within 2 blocks of b; a slot whose mask is 0 holds b. `neighbour_mask`: 0 exactly where slots 1 to 4 fall outside the slab, and at random in slots 5 and 6 (also where they fall outside); slot 0 is always 1.
All inputs are finite; a program needn't handle non-finite values.
Results may differ from a plain program's by a relative error of at most 0.0029.
Values may be sent and summed in bfloat16 or wider, within the bound.
A program may use at most 192 MiB of HBM per device.

v0:
```python
import math

import jax
import jax.numpy as jnp
from jax import lax
from jax.sharding import PartitionSpec as P

REACH = 2


def padded(shard, sides, width):
    for axis, dim in sides:
        count, length = (lax.axis_size(axis), shard.shape[dim])
        up = [(i, (i + 1) % count) for i in range(count - 1)]
        down = [(j, i) for i, j in up]
        last = lax.slice_in_dim(shard, length - width, length, axis=dim)
        leading = lax.slice_in_dim(shard, 0, width, axis=dim)
        before = lax.ppermute(last, axis, up)
        after = lax.ppermute(leading, axis, down)
        shard = jnp.concatenate([before, shard, after], axis=dim)
    return shard


def slot_product(operator_blocks, reduced_basis_tiles, neighbour, coupling_weight):
    sparse_block_list = operator_blocks[:, neighbour]
    operator_product = jnp.einsum(
        "hol,hla->hoa", sparse_block_list, reduced_basis_tiles, preferred_element_type=jnp.float32
    )
    return coupling_weight[:, None, None] * operator_product


def per_device(basis_matrix, operator_blocks, neighbours, neighbour_mask):
    local_rows, column_count = basis_matrix.shape
    block_count, slot_count, half_rows, block_rows = operator_blocks.shape
    weights = neighbour_mask.astype(jnp.float32)
    applied_total_sum = jnp.zeros((block_count, half_rows, column_count), jnp.float32)
    first_slot = 0
    extended = padded(basis_matrix, (("row", 0),), REACH * block_rows)
    rim_tiles = extended.reshape(block_count + 2 * REACH, block_rows, column_count)
    offset_index = neighbours - lax.axis_index("row") * block_count + REACH
    for neighbour in range(first_slot, slot_count):
        selected_entries = jnp.take(rim_tiles, offset_index[:, neighbour], axis=0)
        applied_total_sum = applied_total_sum + slot_product(
            operator_blocks, selected_entries, neighbour, weights[:, neighbour]
        )
    applied_half = applied_total_sum.astype(jnp.bfloat16)
    applied = lax.all_gather(applied_half, "sec", axis=1, tiled=True).reshape(
        local_rows, column_count
    )
    left_width = column_count * lax.axis_size("col") // lax.axis_size("sec")
    everything = lax.all_gather(basis_matrix, "col", axis=1, tiled=True)
    left_projector = lax.dynamic_slice_in_dim(
        everything, lax.axis_index("sec") * left_width, left_width, 1
    )
    scaling = 1.0 / math.sqrt(local_rows * lax.axis_size("row"))
    partial_tile = scaling * lax.dot_general(
        left_projector, applied, (((0,), (0,)), ((), ())), preferred_element_type=jnp.float32
    )
    reduced = lax.psum_scatter(partial_tile, "row", scatter_dimension=0, tiled=True)
    return reduced


def solution(mesh):
    return jax.shard_map(
        per_device,
        mesh=mesh,
        in_specs=(P("row", "col"), P("row", None, "sec", None), P("row", None), P("row", None)),
        out_specs=P(("sec", "row"), "col"),
        check_vma=False,
    )
```

profile of v0, /device:TPU:8, one launch (start us, length us, event | category | flops | bytes accessed | tf_op | source)
XLA Modules:
  0.0 655.2 jit_solution(2696042927453458953)
XLA Ops:
  6.5 0.0 all-gather.5.cloned.1.call-start
  6.5 2.7 fusion.54
  9.3 3.3 collective-permute-start
  12.5 2.6 collective-permute-start.1
  15.2 0.7 convert_element_type.6
  15.9 0.7 subtract_add_fusion
  16.6 42.1 %collective-permute-done = bf16[256,2048]{1,0:T(8,128)(2,1)S(1)} collective-permute-done((bf16[256,2048]{1,0:T(8,128)(2,1)}, bf16[256,2048]{1,0:T(8,128)(2,1)S(1)}, u32[]{:S(2)}, u32[]{:S(2)}) %collective-permute-start) | collective-permute-done | bytes 1048608 | tf_op jit(solution)/shard_map/ppermute | solution.py:18
  58.7 0.0 collective-permute-done.1
  58.7 6.0 pad_maximum_fusion
  64.8 6.9 %gather_fusion.1 = bf16[10,128,2048]{2,1,0:T(8,128)(2,1)} fusion(bf16[14,128,2048]{2,1,0:T(8,128)(2,1)} %bitcast.75, s32[1024]{0:T(1024)S(1)} %get-tuple-element.46), kind=kCustom, calls=%fused_computation.1.clone | custom fusion | bytes 10485800 | tf_op jit(solution)/shard_map/jit(_take)/gather | solution.py:42
  71.7 7.0 %gather_fusion.4 = bf16[10,128,2048]{2,1,0:T(8,128)(2,1)} fusion(bf16[14,128,2048]{2,1,0:T(8,128)(2,1)} %bitcast.76, s32[1024]{0:T(1024)S(1)} %get-tuple-element.43), kind=kCustom, calls=%fused_computation.4.clone | custom fusion | bytes 10485800 | tf_op jit(solution)/shard_map/jit(_take)/gather | solution.py:42
  78.7 7.0 %gather_fusion.3 = bf16[10,128,2048]{2,1,0:T(8,128)(2,1)} fusion(bf16[14,128,2048]{2,1,0:T(8,128)(2,1)} %bitcast.77, s32[1024]{0:T(1024)S(1)} %get-tuple-element.44), kind=kCustom, calls=%fused_computation.3.clone | custom fusion | bytes 10485800 | tf_op jit(solution)/shard_map/jit(_take)/gather | solution.py:42
  85.6 6.9 %gather_fusion.2 = bf16[10,128,2048]{2,1,0:T(8,128)(2,1)} fusion(bf16[14,128,2048]{2,1,0:T(8,128)(2,1)} %bitcast.78, s32[1024]{0:T(1024)S(1)} %get-tuple-element.45), kind=kCustom, calls=%fused_computation.2.clone | custom fusion | bytes 10485800 | tf_op jit(solution)/shard_map/jit(_take)/gather | solution.py:42
  92.5 6.9 %gather_fusion.5 = bf16[10,128,2048]{2,1,0:T(8,128)(2,1)} fusion(bf16[14,128,2048]{2,1,0:T(8,128)(2,1)} %bitcast.79, s32[1024]{0:T(1024)S(1)} %get-tuple-element.42), kind=kCustom, calls=%fused_computation.5.clone | custom fusion | bytes 10485800 | tf_op jit(solution)/shard_map/jit(_take)/gather | solution.py:42
  99.4 6.9 %gather_fusion.6 = bf16[10,128,2048]{2,1,0:T(8,128)(2,1)} fusion(bf16[14,128,2048]{2,1,0:T(8,128)(2,1)} %bitcast.80, s32[1024]{0:T(1024)S(1)} %get-tuple-element.41), kind=kCustom, calls=%fused_computation.6.clone | custom fusion | bytes 10485800 | tf_op jit(solution)/shard_map/jit(_take)/gather | solution.py:42
  106.3 0.0 copy-start
  106.3 7.0 %gather_fusion = bf16[10,128,2048]{2,1,0:T(8,128)(2,1)} fusion(bf16[14,128,2048]{2,1,0:T(8,128)(2,1)} %bitcast.81, s32[1024]{0:T(1024)S(1)} %pad_clamp_fusion.6), kind=kCustom, calls=%fused_computation.clone | custom fusion | bytes 10485800 | tf_op jit(solution)/shard_map/jit(_take)/gather | solution.py:42
  113.4 0.0 copy-done
  113.4 0.0 slice-start.2
  113.4 3.7 fusion.10
  117.1 0.0 slice-start.3
  117.1 0.0 slice-start.4
  117.1 6.1 fusion.4
  123.2 0.0 slice-start.5
  123.2 0.0 slice-done.2
  123.2 0.0 slice-done.3
  123.2 0.0 slice-start
  123.2 3.5 fusion.6
  126.7 0.0 slice-done.4
  126.7 0.0 slice-done.5
  126.7 0.0 slice-start.1
  126.7 0.0 slice-start.6
  126.7 3.4 fusion.8
  130.1 0.0 slice-done
  130.1 0.0 slice-done.1
  130.1 0.0 slice-start.7
  130.1 3.4 fusion.2
  133.4 0.0 slice-done.6
  133.4 0.0 slice-done.7
  133.4 3.4 fusion.12
  136.9 13.9 %fusion.29 = bf16[10,64,2048]{2,1,0:T(8,128)(2,1)} fusion(f32[10]{0:T(128)S(1)} %get-tuple-element.35, f32[10,2048,64]{1,2,0:T(8,128)} %fusion.2, f32[10]{0:T(128)S(1)} %get-tuple-element.36, f32[10,2048,64]{1,2,0:T(8,128)} %fusion.4, f32[10]{0:T(128)S(1)} %get-tuple-element.37, f32[10,2048,64]{1,2,0:T(8,128)} %fusion.6, f32[10]{0:T(128)S(1)} %get-tuple-element.38, ...), kind=kOutput, calls=%fused_computation.39 | convolution fusion | flops 356515840 | bytes 39489536 | tf_op jit(solution)/shard_map/hol,hla->hoa/dot_general | solution.py:26
  150.8 0.0 all-gather.5.cloned.1.call-update
  150.8 0.0 all-gather.3.cloned.1.call-start
  150.9 0.7 all-gather.3.cloned.1.call-update
  151.6 0.0 reduce-scatter.2.cloned.1.call-start
  151.6 77.4 %all-gather.5.cloned.1.call-done = bf16[10,128,2048]{2,1,0:T(8,128)(2,1)} async-done(((bf16[10,64,2048]{2,1,0:T(8,128)(2,1)}), bf16[10,128,2048]{2,1,0:T(8,128)(2,1)}) %all-gather.5.cloned.1.call-update) | async-done | bytes 5242896 | tf_op jit(solution)/shard_map/all_gather | solution.py:47
  229.0 30.4 %all-gather.3.cloned.1.call-done = bf16[1280,4096]{1,0:T(8,128)(2,1)} async-done(((bf16[1280,2048]{1,0:T(8,128)(2,1)}), bf16[1280,4096]{1,0:T(8,128)(2,1)}) %all-gather.3.cloned.1.call-update) | async-done | bytes 10485776 | tf_op jit(solution)/shard_map/all_gather | solution.py:51
  259.4 17.9 %convolution_multiply_fusion = f32[2048,2048]{1,0:T(8,128)} fusion(bf16[1280,2048]{1,0:T(8,128)(2,1)} %bitcast.90, bf16[1280,4096]{1,0:T(8,128)(2,1)} %all-gather.3.cloned.1.call-done, s32[]{:T(128)S(6)} %select_n.10), kind=kOutput, calls=%fused_computation.7 | convolution fusion | flops 10741612544 | bytes 27262980 | tf_op jit(solution)/shard_map/dot_general | solution.py:56
  277.3 0.0 reduce-scatter.2.cloned.1.call-update
  277.3 371.3 %reduce-scatter.2.cloned.1.call-done = f32[32,2048]{1,0:T(8,128)} async-done(((f32[2048,2048]{1,0:T(8,128)}), f32[32,2048]{1,0:T(8,128)}) %reduce-scatter.2.cloned.1.call-update) | async-done | bytes 262160 | tf_op jit(solution)/shard_map/reduce_scatter | solution.py:59
  (10 shorter events, 0.1 us)
Async XLA Ops:
  6.5 222.5 %all-gather.5.cloned.1.call-start = ((), (), s32[]{:S(2)}) async-start(), calls=%async_computation.2 | async-start | bytes 7864320 | tf_op jit(solution)/shard_map/all_gather | solution.py:47
  9.3 49.5 %collective-permute-start = (bf16[256,2048]{1,0:T(8,128)(2,1)}, bf16[256,2048]{1,0:T(8,128)(2,1)S(1)}, u32[]{:S(2)}, u32[]{:S(2)}) collective-permute-start(bf16[256,2048]{1,0:T(8,128)(2,1)} %get-tuple-element.20), channel_id=1, source_target_pairs={{0,2},{2,4},{4,6},{6,8},{8,10},{10,12},{12,14},{14,16},{16,18},{18... | collective-permute-start | bytes 3145736 | tf_op jit(solution)/shard_map/ppermute | solution.py:18
  12.5 46.2 %collective-permute-start.1 = (bf16[256,2048]{1,0:T(8,128)(2,1)S(1)}, bf16[256,2048]{1,0:T(8,128)(2,1)S(1)}, u32[]{:S(2)}, u32[]{:S(2)}) collective-permute-start(bf16[256,2048]{1,0:T(8,128)(2,1)S(1)} %get-tuple-element.21), channel_id=1, source_target_pairs={{2,0},{4,2},{6,4},{8,6},{10,8},{12,10},{14,12},{16,14},{18,16},{20... | collective-permute-start | bytes 3145736 | tf_op jit(solution)/shard_map/ppermute | solution.py:19
  106.3 7.0 %copy-start = (bf16[10,7,64,128]{3,2,1,0:T(8,128)(2,1)S(1)}, bf16[10,7,64,128]{3,2,1,0:T(8,128)(2,1)}, u32[]{:S(2)}) copy-start(bf16[10,7,64,128]{3,2,1,0:T(8,128)(2,1)} %param.7) | copy-start | bytes 3440644
  113.4 9.8 %slice-start.2 = ((s8[5242880]{0:T(1024)(128)(4,1)}), s8[4194304]{0:T(1024)(128)(4,1)S(1)}, s32[]{:S(2)}) async-start(s8[5242880]{0:T(1024)(128)(4,1)} %bitcast.84), calls=%async_computation.6 | async-start | bytes 8388608
  117.1 6.1 slice-start.3
  117.1 9.6 %slice-start.4 = ((s8[5242880]{0:T(1024)(128)(4,1)}), s8[4194304]{0:T(1024)(128)(4,1)S(1)}, s32[]{:S(2)}) async-start(s8[5242880]{0:T(1024)(128)(4,1)} %bitcast.86), calls=%async_computation.8 | async-start | bytes 8388608
  123.2 3.5 slice-start.5
  123.2 6.9 %slice-start = ((s8[5242880]{0:T(1024)(128)(4,1)}), s8[4194304]{0:T(1024)(128)(4,1)S(1)}, s32[]{:S(2)}) async-start(s8[5242880]{0:T(1024)(128)(4,1)} %bitcast.82), calls=%async_computation.4 | async-start | bytes 8388608
  126.7 3.4 slice-start.1
  126.7 6.8 %slice-start.6 = ((s8[5242880]{0:T(1024)(128)(4,1)}), s8[4194304]{0:T(1024)(128)(4,1)S(1)}, s32[]{:S(2)}) async-start(s8[5242880]{0:T(1024)(128)(4,1)} %bitcast.88), calls=%async_computation.10 | async-start | bytes 8388608
  130.1 3.4 slice-start.7
  150.8 108.6 %all-gather.3.cloned.1.call-start = ((), (), s32[]{:S(2)}) async-start(), calls=%async_computation.1 | async-start | bytes 15728640 | tf_op jit(solution)/shard_map/all_gather | solution.py:51
  151.6 497.1 %reduce-scatter.2.cloned.1.call-start = ((), (), s32[]{:S(2)}) async-start(), calls=%async_computation.3 | async-start | bytes 17039360 | tf_op jit(solution)/shard_map/reduce_scatter | solution.py:59
Sparse Core Ops, SparseCore 0:
  150.9 78.0 all-gather.4
  230.8 28.5 all-gather.2
  277.4 371.1 reduce-scatter.1
where the time goes:
time: 658 us; the launch traced here: 655 us
  waiting for transfers between devices  522 us (79%)
  matrix products  55.2 us (8%)
  local copies, waits for them, and re-layouts  51.4 us (8%)
  between operations  13.2 us (2%)
  other arithmetic  7.46 us (1%)
    reduce_scatter x1, waiting for transfers between devices, per_device(): lax.psum_scatter(partial_tile, 'row', scatter_dimension=0, tiled=True)  371 us
    all_gather x1, waiting for transfers between devices, per_device(): lax.all_gather(applied_half, 'sec', axis=1, tiled=True)  77.4 us
    gather x7, local copies, waits for them, and re-layouts, per_device(): selected_entries = jnp.take(rim_tiles, offset_index[:, neighbour], axis=0)  48.6 us
    ppermute x1, waiting for transfers between devices, padded(): before = lax.ppermute(last, axis, up)  42.1 us
    dot_general x7, matrix products, slot_product(): jnp.einsum('hol,hla->hoa', sparse_block_list, reduced_basis_tiles, prefer...  37.3 us
    all_gather x1, waiting for transfers between devices, per_device(): everything = lax.all_gather(basis_matrix, 'col', axis=1, tiled=True)  30.4 us
    dot_general x1, matrix products, per_device(): lax.dot_general(left_projector, applied, (((0,), (0,)), ((), ())), prefer...  17.9 us
  transfers between devices with their start and end apart: 5, of which 4 were waited for; matrix products, arithmetic and copies ran while one was open for 0% of the time, Pallas kernels for 0%

commit v1 on v0

v1 whole, which is shorter than its diff:
```python
import math

import jax
import jax.numpy as jnp
import numpy as np
from jax import lax
from jax.sharding import Mesh
from jax.sharding import PartitionSpec as P

REACH = 2
ROW_PARTS = (("z", 8), ("x", 4), ("y", 2))
ROW = tuple(name for name, _ in ROW_PARTS)
STATIC_OFFSETS = (0, -1, 1, -2, 2)


def halo(shard, width):
    count = 1
    for _, size in ROW_PARTS:
        count *= size
    length = shard.shape[0]
    up = [(i, i + 1) for i in range(count - 1)]
    down = [(j, i) for i, j in up]
    before = lax.ppermute(shard[length - width :], ROW, up)
    after = lax.ppermute(shard[:width], ROW, down)
    return jnp.concatenate([before, shard, after], axis=0)


def take_chunk(x, index, dim):
    return lax.dynamic_index_in_dim(x, index, axis=dim, keepdims=False)


def ring_sum(x, dim, axis, n):
    p = lax.axis_index(axis)
    if n == 2:
        partner = [(0, 1), (1, 0)]
        got = lax.ppermute(take_chunk(x, 1 - p, dim), axis, partner)
        return got + take_chunk(x, p, dim)
    half = x.shape[-1] // 2
    forward, backward = x[..., :half], x[..., half:]
    right = [(i, (i + 1) % n) for i in range(n)]
    left = [(i, (i - 1) % n) for i in range(n)]
    acc_f = take_chunk(forward, (p - 1) % n, dim)
    acc_b = take_chunk(backward, (p + 1) % n, dim)
    for step in range(1, n):
        got_f = lax.ppermute(acc_f, axis, right)
        got_b = lax.ppermute(acc_b, axis, left)
        acc_f = got_f + take_chunk(forward, (p - step - 1) % n, dim)
        acc_b = got_b + take_chunk(backward, (p + step + 1) % n, dim)
    return jnp.concatenate([acc_f, acc_b], axis=-1)


def per_device(basis_matrix, operator_blocks, neighbours, neighbour_mask):
    local_rows, column_count = basis_matrix.shape
    block_count, slot_count, half_rows, block_rows = operator_blocks.shape
    sec = lax.axis_index("sec")
    col = lax.axis_index("col")
    row = 0
    for name, size in ROW_PARTS:
        row = row * size + lax.axis_index(name)

    other_half = lax.ppermute(operator_blocks, "sec", [(0, 1), (1, 0)])
    first = jnp.where(sec == 0, operator_blocks, other_half)
    second = jnp.where(sec == 0, other_half, operator_blocks)
    full_ops = jnp.concatenate([first, second], axis=2)

    other_basis = lax.ppermute(basis_matrix, "col", [(0, 1), (1, 0)])
    left_projector = jnp.where(sec == col, basis_matrix, other_basis)

    weights = neighbour_mask.astype(jnp.float32)
    extended = halo(basis_matrix, REACH * block_rows)
    tiles = extended.reshape(block_count + 2 * REACH, block_rows, column_count)
    applied = jnp.zeros((block_count, block_rows, column_count), jnp.float32)
    for slot in range(slot_count):
        if slot < len(STATIC_OFFSETS):
            start = REACH + STATIC_OFFSETS[slot]
            selected = tiles[start : start + block_count]
        else:
            offset_index = neighbours[:, slot] - row * block_count + REACH
            selected = jnp.take(tiles, offset_index, axis=0)
        product = jnp.einsum(
            "hol,hla->hoa", full_ops[:, slot], selected, preferred_element_type=jnp.float32
        )
        applied = applied + weights[:, slot][:, None, None] * product
    applied = applied.astype(jnp.bfloat16).reshape(local_rows, column_count)

    row_count = 1
    for _, size in ROW_PARTS:
        row_count *= size
    scaling = 1.0 / math.sqrt(local_rows * row_count)
    partial_tile = scaling * lax.dot_general(
        left_projector, applied, (((0,), (0,)), ((), ())), preferred_element_type=jnp.float32
    )
    chunk_rows = partial_tile.shape[0] // row_count
    shape = tuple(size for _, size in ROW_PARTS) + (chunk_rows, column_count)
    partial = partial_tile.reshape(shape)
    for name, size in ROW_PARTS:
        partial = ring_sum(partial, 0, name, size)
    return partial


def solution(mesh):
    sizes = [mesh.shape["sec"]] + [size for _, size in ROW_PARTS] + [mesh.shape["col"]]
    fine = Mesh(np.asarray(mesh.devices).reshape(sizes), ("sec",) + ROW + ("col",))
    return jax.shard_map(
        per_device,
        mesh=fine,
        in_specs=(P(ROW, "col"), P(ROW, None, "sec", None), P(ROW, None), P(ROW, None)),
        out_specs=P(("sec",) + ROW, "col"),
        check_vma=False,
    )
```

time: 658 us -> 427 us (0.65)
  waiting for transfers between devices: 522 us -> 204 us
  starting transfers between devices: 5.97 us -> 46.1 us
  other arithmetic: 7.46 us -> 31.4 us
  matrix products: 55.2 us -> 76.3 us
  local copies, waits for them, and re-layouts: 51.4 us -> 64.8 us
  between operations: 13.2 us -> 0.87 us
    reduce_scatter x1 -> x0, waiting for transfers between devices: 371 us -> none  [per_device(): lax.psum_scatter(partial_tile, 'row', scatter_dimension=0, tiled=True)]
    ppermute x2 -> x25, waiting for transfers between devices: 42.1 us -> 204 us  [the longest x10 138 us: ring_sum(): got_b = lax.ppermute(acc_b, axis, left)]
    all_gather x2 -> x0, waiting for transfers between devices: 108 us -> none  [the longest x1 77.4 us: per_device(): lax.all_gather(applied_half, 'sec', axis=1, tiled=True)]
    ppermute x2 -> x25, starting transfers between devices: 5.89 us -> 46.1 us  [the longest x10 34.1 us: ring_sum(): got_b = lax.ppermute(acc_b, axis, left)]
    gather x7 -> x2, local copies, waits for them, and re-layouts: 48.6 us -> 14.4 us  [per_device(): selected = jnp.take(tiles, offset_index, axis=0)]
    slice x1 -> x4, local copies, waits for them, and re-layouts: 2.72 us -> 32.9 us  [the longest x2 20.4 us: per_device(): selected = tiles[start:start + block_count]]
    add x1 -> x21, other arithmetic: 0.69 us -> 24.4 us  [the longest x10 12.5 us: ring_sum(): acc_b = got_b + take_chunk(backward, (p + step + 1) % n, dim)]
    dot_general x7, matrix products: 37.3 us -> 59.8 us  [per_device(): jnp.einsum('hol,hla->hoa', full_ops[:, slot], selected, preferred_element...]
  transfers between devices with their start and end apart: 5 -> 25, of which waited for: 4 -> 16; matrix products, arithmetic and copies ran while one was open for 0% -> 33% of each run, Pallas kernels for 0% -> 0%
where the time goes in v1:
time: 427 us; the launch traced here: 423 us
  waiting for transfers between devices  204 us (48%)
  matrix products  76.3 us (18%)
  local copies, waits for them, and re-layouts  64.8 us (15%)
  starting transfers between devices  46.1 us (11%)
  other arithmetic  31.4 us (7%)
    ppermute x10, waiting for transfers between devices, ring_sum(): got_b = lax.ppermute(acc_b, axis, left)  138 us
    dot_general x7, matrix products, per_device(): jnp.einsum('hol,hla->hoa', full_ops[:, slot], selected, preferred_element...  59.8 us
    ppermute x1, waiting for transfers between devices, halo(): before = lax.ppermute(shard[length - width:], ROW, up)  39 us
    ppermute x10, starting transfers between devices, ring_sum(): got_b = lax.ppermute(acc_b, axis, left)  34.1 us
    ppermute x10, waiting for transfers between devices, ring_sum(): got_f = lax.ppermute(acc_f, axis, right)  22.6 us
    slice x2, local copies, waits for them, and re-layouts, per_device(): selected = tiles[start:start + block_count]  20.4 us
    dot_general x1, matrix products, per_device(): lax.dot_general(left_projector, applied, (((0,), (0,)), ((), ())), prefer...  16.5 us
    gather x2, local copies, waits for them, and re-layouts, per_device(): selected = jnp.take(tiles, offset_index, axis=0)  14.4 us
  transfers between devices with their start and end apart: 25, of which 16 were waited for; matrix products, arithmetic and copies ran while one was open for 33% of the time, Pallas kernels for 0%

profile of v1, /device:TPU:8, one launch (start us, length us, event | category | flops | bytes accessed | tf_op | source)
XLA Modules:
  0.0 423.3 jit_solution(4497036512025706809)
XLA Ops:
  0.0 3.2 fusion.55
  3.2 3.3 collective-permute-start.2
  6.4 2.6 collective-permute-start.3
  9.2 2.4 copy.6
  11.6 2.3 collective-permute-start.1
  13.9 0.8 compare_and_fusion
  14.7 39.0 %collective-permute-done.2 = bf16[256,2048]{1,0:T(8,128)(2,1)S(1)} collective-permute-done((bf16[256,2048]{1,0:T(8,128)(2,1)}, bf16[256,2048]{1,0:T(8,128)(2,1)S(1)}, u32[]{:S(2)}, u32[]{:S(2)}) %collective-permute-start.2) | collective-permute-done | bytes 1048608 | tf_op jit(solution)/shard_map/ppermute | solution.py:23
  53.8 6.0 %pad_maximum_fusion = bf16[1792,2048]{1,0:T(8,128)(2,1)} fusion(bf16[256,2048]{1,0:T(8,128)(2,1)S(1)} %collective-permute-done.3, bf16[1280,2048]{1,0:T(8,128)(2,1)} %param.6, bf16[256,2048]{1,0:T(8,128)(2,1)S(1)} %collective-permute-done.2), kind=kLoop, calls=%fused_computation.4 | loop fusion | flops 22020096 | bytes 14680064 | tf_op jit(solution)/shard_map/concatenate | solution.py:25
  59.8 6.9 %gather_fusion = bf16[10,128,2048]{2,1,0:T(8,128)(2,1)} fusion(bf16[14,128,2048]{2,1,0:T(8,128)(2,1)} %bitcast.112, s32[1024]{0:T(1024)S(1)} %get-tuple-element.32), kind=kCustom, calls=%fused_computation.clone | custom fusion | bytes 10485800 | tf_op jit(solution)/shard_map/jit(_take)/gather | solution.py:79
  66.7 7.5 %gather_fusion.1 = bf16[10,128,2048]{2,1,0:T(8,128)(2,1)} fusion(bf16[14,128,2048]{2,1,0:T(8,128)(2,1)} %bitcast.113, s32[1024]{0:T(1024)S(1)} %get-tuple-element.31), kind=kCustom, calls=%fused_computation.1.clone | custom fusion | bytes 10485800 | tf_op jit(solution)/shard_map/jit(_take)/gather | solution.py:79
  74.2 1.0 constant_dynamic-update-slice_fusion.1
  75.2 8.1 %constant_dynamic-update-slice_fusion = (bf16[1536,2048]{1,0:T(8,128)(2,1)}, bf16[1536,2048]{1,0:T(8,128)(2,1)}) fusion(bf16[1536,2048]{1,0:T(8,128)(2,1)} %constant_dynamic-update-slice_fusion.1, bf16[1280,2048]{1,0:T(8,128)(2,1)} %param.6), kind=kLoop, calls=%fused_computation.82 | loop fusion | bytes 15728640 | tf_op jit(solution)/shard_map/concatenate | solution.py:25
  83.4 1.1 constant_dynamic-update-slice_fusion.2
  84.4 10.2 %fusion.54 = (bf16[1280,2048]{1,0:T(8,128)(2,1)}, bf16[1280,2048]{1,0:T(8,128)(2,1)}) fusion(bf16[1536,2048]{1,0:T(8,128)(2,1)} %constant_dynamic-update-slice_fusion.2), kind=kLoop, calls=%fused_computation.110 | loop fusion | bytes 20971520 | tf_op jit(solution)/shard_map/slice | solution.py:76
  94.6 10.2 %fusion.53 = (bf16[1280,2048]{1,0:T(8,128)(2,1)}, bf16[1280,2048]{1,0:T(8,128)(2,1)}) fusion(bf16[1536,2048]{1,0:T(8,128)(2,1)} %get-tuple-element.16), kind=kLoop, calls=%fused_computation.109 | loop fusion | bytes 20971520 | tf_op jit(solution)/shard_map/slice | solution.py:76
  105.0 8.2 %fusion.22 = f32[10,128,2048]{2,1,0:T(8,128)} fusion(bf16[10,128,2048]{2,1,0:T(8,128)(2,1)} %bitcast.120, bf16[10,7,64,128]{3,2,0,1:T(8,128)(2,1)S(1)} %get-tuple-element.21, bf16[10,7,64,128]{3,2,0,1:T(8,128)(2,1)S(1)} %get-tuple-element.20), kind=kOutput, calls=%fused_computation.59 | convolution fusion | flops 671744000 | bytes 18022400 | tf_op jit(solution)/shard_map/hol,hla->hoa/dot_general | solution.py:80
  113.2 5.4 %fusion.26 = f32[10,128,2048]{2,1,0:T(8,128)} fusion(bf16[10,128,2048]{2,1,0:T(8,128)(2,1)S(1)} %bitcast.116, bf16[10,7,64,128]{3,2,0,1:T(8,128)(2,1)S(1)} %get-tuple-element.21, bf16[10,7,64,128]{3,2,0,1:T(8,128)(2,1)S(1)} %get-tuple-element.20), kind=kOutput, calls=%fused_computation.63 | convolution fusion | flops 671744000 | bytes 18022400 | tf_op jit(solution)/shard_map/hol,hla->hoa/dot_general | solution.py:80
  118.7 6.4 %fusion.24 = f32[10,128,2048]{2,1,0:T(8,128)} fusion(bf16[10,128,2048]{2,1,0:T(8,128)(2,1)S(1)} %bitcast.123, bf16[10,7,64,128]{3,2,0,1:T(8,128)(2,1)S(1)} %get-tuple-element.21, bf16[10,7,64,128]{3,2,0,1:T(8,128)(2,1)S(1)} %get-tuple-element.20), kind=kOutput, calls=%fused_computation.61 | convolution fusion | flops 671744000 | bytes 18022400 | tf_op jit(solution)/shard_map/hol,hla->hoa/dot_general | solution.py:80
  125.1 5.4 %fusion.28 = f32[10,128,2048]{2,1,0:T(8,128)} fusion(bf16[10,128,2048]{2,1,0:T(8,128)(2,1)S(1)} %bitcast.119, bf16[10,7,64,128]{3,2,0,1:T(8,128)(2,1)S(1)} %get-tuple-element.21, bf16[10,7,64,128]{3,2,0,1:T(8,128)(2,1)S(1)} %get-tuple-element.20), kind=kOutput, calls=%fused_computation.65 | convolution fusion | flops 671744000 | bytes 18022400 | tf_op jit(solution)/shard_map/hol,hla->hoa/dot_general | solution.py:80
  130.5 5.5 %fusion.30 = f32[10,128,2048]{2,1,0:T(8,128)} fusion(bf16[10,128,2048]{2,1,0:T(8,128)(2,1)S(1)} %bitcast.111, bf16[10,7,64,128]{3,2,0,1:T(8,128)(2,1)S(1)} %get-tuple-element.21, bf16[10,7,64,128]{3,2,0,1:T(8,128)(2,1)S(1)} %get-tuple-element.20), kind=kOutput, calls=%fused_computation.67 | convolution fusion | flops 671744000 | bytes 18022400 | tf_op jit(solution)/shard_map/hol,hla->hoa/dot_general | solution.py:80
  136.1 5.7 %fusion.2 = f32[10,128,2048]{2,1,0:T(8,128)} fusion(bf16[10,128,2048]{2,1,0:T(8,128)(2,1)S(1)} %bitcast.127, pred[10]{0:T(512)(128)(4,1)S(1)} %get-tuple-element.22, bf16[10,7,64,128]{3,2,0,1:T(8,128)(2,1)S(1)} %get-tuple-element.21, bf16[10,7,64,128]{3,2,0,1:T(8,128)(2,1)S(1)} %get-tuple-element.20), kind=kOutput, calls=%fused_computation.7 | convolution fusion | flops 674365440 | bytes 18022410 | tf_op jit(solution)/shard_map/hol,hla->hoa/dot_general | solution.py:80
  141.8 23.1 %add_convert_fusion = bf16[10,128,2048]{2,1,0:T(8,128)(2,1)} fusion(f32[10,128,2048]{2,1,0:T(8,128)} %fusion.2, f32[10,128,2048]{2,1,0:T(8,128)} %fusion.22, f32[10,128,2048]{2,1,0:T(8,128)} %fusion.24, f32[10,128,2048]{2,1,0:T(8,128)} %fusion.26, f32[10,128,2048]{2,1,0:T(8,128)} %fusion.28, f32[10,128,2048]{2,1,0:T(8,128)} %fusion.30, ...), kind=kOutput, calls=%fused_computation.2 | convolution fusion | flops 711065600 | bytes 75694368 | tf_op jit(solution)/shard_map/hol,hla->hoa/dot_general | solution.py:80
  164.9 16.5 %convolution_multiply_fusion = f32[2048,2048]{1,0:T(8,128)} fusion(bf16[1280,2048]{1,0:T(8,128)(2,1)} %bitcast.129, bf16[1280,2048]{1,0:T(8,128)(2,1)S(1)} %bitcast.110, bf16[1280,2048]{1,0:T(8,128)(2,1)} %collective-permute-done, pred[]{:T(512)S(6)} %eq.32), kind=kOutput, calls=%fused_computation.3 | convolution fusion | flops 10744233984 | bytes 32505856 | tf_op jit(solution)/shard_map/dot_general | solution.py:90
  181.4 9.4 %fusion.52 = (f32[8,4,2,32,1024]{4,3,2,1,0:T(8,128)S(1)}, f32[8,4,2,32,1024]{4,3,2,1,0:T(8,128)}) fusion(f32[8,4,2,32,2048]{4,3,2,1,0:T(8,128)} %bitcast.128), kind=kLoop, calls=%fused_computation.108 | loop fusion | bytes 33554432 | tf_op jit(solution)/shard_map/slice | solution.py:39
  190.8 3.3 copy-done
  194.2 6.0 %collective-permute-start.14 = (f32[4,2,32,1024]{3,2,1,0:T(8,128)S(1)}, f32[4,2,32,1024]{3,2,1,0:T(8,128)}, u32[]{:S(2)}, u32[]{:S(2)}) collective-permute-start(f32[4,2,32,1024]{3,2,1,0:T(8,128)S(1)} %dynamic-slice_bitcast_fusion), channel_id=1, source_target_pairs={{0,112},{16,0},{32,16},{48,32},{64,48},{80,64},{96,80},{112,96},{1... | collective-permute-start | bytes 3145736 | tf_op jit(solution)/shard_map/ppermute | solution.py:46
  200.1 1.3 dynamic-slice_bitcast_fusion.1
  201.5 21.7 %collective-permute-done.14 = f32[4,2,32,1024]{3,2,1,0:T(8,128)} collective-permute-done((f32[4,2,32,1024]{3,2,1,0:T(8,128)S(1)}, f32[4,2,32,1024]{3,2,1,0:T(8,128)}, u32[]{:S(2)}, u32[]{:S(2)}) %collective-permute-start.14) | collective-permute-done | bytes 1048608 | tf_op jit(solution)/shard_map/ppermute | solution.py:46
  223.3 1.7 bitcast_add_fusion.6
  224.9 3.9 collective-permute-start.15
  228.8 1.4 bitcast_add_fusion.13
  230.5 21.2 %collective-permute-done.15 = f32[4,2,32,1024]{3,2,1,0:T(8,128)} collective-permute-done((f32[4,2,32,1024]{3,2,1,0:T(8,128)S(1)}, f32[4,2,32,1024]{3,2,1,0:T(8,128)}, u32[]{:S(2)}, u32[]{:S(2)}) %collective-permute-start.15) | collective-permute-done | bytes 1048608 | tf_op jit(solution)/shard_map/ppermute | solution.py:46
  251.7 1.7 bitcast_add_fusion.5
  253.3 3.9 collective-permute-start.16
  257.2 1.4 bitcast_add_fusion.12
  258.7 20.6 %collective-permute-done.16 = f32[4,2,32,1024]{3,2,1,0:T(8,128)} collective-permute-done((f32[4,2,32,1024]{3,2,1,0:T(8,128)S(1)}, f32[4,2,32,1024]{3,2,1,0:T(8,128)}, u32[]{:S(2)}, u32[]{:S(2)}) %collective-permute-start.16) | collective-permute-done | bytes 1048608 | tf_op jit(solution)/shard_map/ppermute | solution.py:46
  279.2 1.7 bitcast_add_fusion.4
  280.9 3.9 collective-permute-start.17
  284.8 1.4 bitcast_add_fusion.11
  286.3 19.6 %collective-permute-done.17 = f32[4,2,32,1024]{3,2,1,0:T(8,128)} collective-permute-done((f32[4,2,32,1024]{3,2,1,0:T(8,128)S(1)}, f32[4,2,32,1024]{3,2,1,0:T(8,128)}, u32[]{:S(2)}, u32[]{:S(2)}) %collective-permute-start.17) | collective-permute-done | bytes 1048608 | tf_op jit(solution)/shard_map/ppermute | solution.py:46
  305.9 1.7 bitcast_add_fusion.3
  307.6 3.9 collective-permute-start.18
  311.5 1.4 bitcast_add_fusion.10
  312.9 18.7 %collective-permute-done.18 = f32[4,2,32,1024]{3,2,1,0:T(8,128)} collective-permute-done((f32[4,2,32,1024]{3,2,1,0:T(8,128)S(1)}, f32[4,2,32,1024]{3,2,1,0:T(8,128)}, u32[]{:S(2)}, u32[]{:S(2)}) %collective-permute-start.18) | collective-permute-done | bytes 1048608 | tf_op jit(solution)/shard_map/ppermute | solution.py:46
  331.7 1.7 bitcast_add_fusion.2
  333.3 3.9 collective-permute-start.19
  337.2 2.3 bitcast_add_fusion.9
  339.5 16.9 %collective-permute-done.19 = f32[4,2,32,1024]{3,2,1,0:T(8,128)} collective-permute-done((f32[4,2,32,1024]{3,2,1,0:T(8,128)S(1)}, f32[4,2,32,1024]{3,2,1,0:T(8,128)}, u32[]{:S(2)}, u32[]{:S(2)}) %collective-permute-start.19) | collective-permute-done | bytes 1048608 | tf_op jit(solution)/shard_map/ppermute | solution.py:46
  356.5 1.7 bitcast_add_fusion.1
  358.2 3.9 collective-permute-start.20
  362.5 1.7 bitcast_add_fusion.8
  364.4 16.0 %collective-permute-done.20 = f32[4,2,32,1024]{3,2,1,0:T(8,128)S(1)} collective-permute-done((f32[4,2,32,1024]{3,2,1,0:T(8,128)S(1)}, f32[4,2,32,1024]{3,2,1,0:T(8,128)S(1)}, u32[]{:S(2)}, u32[]{:S(2)}) %collective-permute-start.20) | collective-permute-done | bytes 1048608 | tf_op jit(solution)/shard_map/ppermute | solution.py:46
  380.4 1.4 bitcast_add_fusion
  382.5 3.7 collective-permute-done.10
  386.1 1.7 bitcast_add_fusion.7
  388.0 2.4 collective-permute-done.21
  390.4 1.0 bitcast_add_fusion.16
  391.4 0.9 collective-permute-start.22
  392.2 5.8 %collective-permute-done.11 = f32[2,32,1024]{2,1,0:T(8,128)S(1)} collective-permute-done((f32[2,32,1024]{2,1,0:T(8,128)S(1)}, f32[2,32,1024]{2,1,0:T(8,128)S(1)}, u32[]{:S(2)}, u32[]{:S(2)}) %collective-permute-start.11) | collective-permute-done | bytes 262176 | tf_op jit(solution)/shard_map/ppermute | solution.py:45
  399.2 3.4 collective-permute-start.23
  402.6 5.1 %collective-permute-done.12 = f32[2,32,1024]{2,1,0:T(8,128)S(1)} collective-permute-done((f32[2,32,1024]{2,1,0:T(8,128)S(1)}, f32[2,32,1024]{2,1,0:T(8,128)S(1)}, u32[]{:S(2)}, u32[]{:S(2)}) %collective-permute-start.12) | collective-permute-done | bytes 262176 | tf_op jit(solution)/shard_map/ppermute | solution.py:45
  407.9 7.5 %collective-permute-done.13 = f32[2,32,1024]{2,1,0:T(8,128)S(1)} collective-permute-done((f32[2,32,1024]{2,1,0:T(8,128)S(1)}, f32[2,32,1024]{2,1,0:T(8,128)S(1)}, u32[]{:S(2)}, u32[]{:S(2)}) %collective-permute-start.13) | collective-permute-done | bytes 262176 | tf_op jit(solution)/shard_map/ppermute | solution.py:45
  415.4 2.5 collective-permute-start.24
  417.9 4.4 %collective-permute-done.24 = f32[32,2048]{1,0:T(8,128)S(1)} collective-permute-done((f32[32,2048]{1,0:T(8,128)S(1)}, f32[32,2048]{1,0:T(8,128)S(1)}, u32[]{:S(2)}, u32[]{:S(2)}) %collective-permute-start.24) | collective-permute-done | bytes 262176 | tf_op jit(solution)/shard_map/ppermute | solution.py:36
  (72 shorter events, 4.6 us)
Async XLA Ops:
  0.0 13.9 %copy-start.2 = (s32[10,7]{0,1:T(8,128)S(1)}, s32[10,7]{0,1:T(8,128)}, u32[]{:S(2)}) copy-start(s32[10,7]{0,1:T(8,128)} %param.9) | copy-start | bytes 844
  3.2 50.6 %collective-permute-start.2 = (bf16[256,2048]{1,0:T(8,128)(2,1)}, bf16[256,2048]{1,0:T(8,128)(2,1)S(1)}, u32[]{:S(2)}, u32[]{:S(2)}) collective-permute-start(bf16[256,2048]{1,0:T(8,128)(2,1)} %get-tuple-element.18), channel_id=1, source_target_pairs={{0,2},{2,4},{4,6},{6,8},{8,10},{10,12},{12,14},{14,16},{16,18},{18... | collective-permute-start | bytes 3145736 | tf_op jit(solution)/shard_map/ppermute | solution.py:23
  6.4 47.3 %collective-permute-start.3 = (bf16[256,2048]{1,0:T(8,128)(2,1)}, bf16[256,2048]{1,0:T(8,128)(2,1)S(1)}, u32[]{:S(2)}, u32[]{:S(2)}) collective-permute-start(bf16[256,2048]{1,0:T(8,128)(2,1)} %get-tuple-element.19), channel_id=1, source_target_pairs={{2,0},{4,2},{6,4},{8,6},{10,8},{12,10},{14,12},{16,14},{18,16},{20... | collective-permute-start | bytes 3145736 | tf_op jit(solution)/shard_map/ppermute | solution.py:24
  9.1 155.9 %collective-permute-start = (bf16[1280,2048]{1,0:T(8,128)(2,1)}, bf16[1280,2048]{1,0:T(8,128)(2,1)}, u32[]{:S(2)}, u32[]{:S(2)}) collective-permute-start(bf16[1280,2048]{1,0:T(8,128)(2,1)} %param.6), channel_id=1, source_target_pairs={{0,1},{1,0},{2,3},{3,2},{4,5},{5,4},{6,7},{7,6},{8,9},{9,8},{10,11... | collective-permute-start | bytes 15728648 | tf_op jit(solution)/shard_map/ppermute | solution.py:66
  11.6 93.2 %collective-permute-start.1 = (bf16[10,7,64,128]{3,2,0,1:T(8,128)(2,1)}, bf16[10,7,64,128]{3,2,0,1:T(8,128)(2,1)S(1)}, u32[]{:S(2)}, u32[]{:S(2)}) collective-permute-start(bf16[10,7,64,128]{3,2,0,1:T(8,128)(2,1)} %copy.6), channel_id=1, source_target_pairs={{0,128},{128,0},{1,129},{129,1},{2,130},{130,2},{3,131},{131,3},{4... | collective-permute-start | bytes 3440648 | tf_op jit(solution)/shard_map/ppermute | solution.py:61
  94.6 10.2 %copy-start.1 = (bf16[10,7,64,128]{3,2,1,0:T(8,128)(2,1)S(1)}, bf16[10,7,64,128]{3,2,1,0:T(8,128)(2,1)}, u32[]{:S(2)}) copy-start(bf16[10,7,64,128]{3,2,1,0:T(8,128)(2,1)} %param.7) | copy-start | bytes 3440644
  105.0 8.2 %slice-start.2 = ((s8[5242880]{0:T(1024)(128)(4,1)}), s8[4194304]{0:T(1024)(128)(4,1)S(1)}, s32[]{:S(2)}) async-start(s8[5242880]{0:T(1024)(128)(4,1)} %bitcast.114), calls=%async_computation.2 | async-start | bytes 8388608
  105.0 8.2 %slice-start.3 = ((s8[5242880]{0:T(1024)(128)(4,1)}), s8[1048576]{0:T(1024)(128)(4,1)S(1)}, s32[]{:S(2)}) async-start(s8[5242880]{0:T(1024)(128)(4,1)} %bitcast.114), calls=%async_computation.3 | async-start | bytes 2097152
  113.2 5.4 %slice-start.6 = ((s8[5242880]{0:T(1024)(128)(4,1)}), s8[4194304]{0:T(1024)(128)(4,1)S(1)}, s32[]{:S(2)}) async-start(s8[5242880]{0:T(1024)(128)(4,1)} %bitcast.121), calls=%async_computation.6 | async-start | bytes 8388608
  113.2 5.4 %slice-start.7 = ((s8[5242880]{0:T(1024)(128)(4,1)}), s8[1048576]{0:T(1024)(128)(4,1)S(1)}, s32[]{:S(2)}) async-start(s8[5242880]{0:T(1024)(128)(4,1)} %bitcast.121), calls=%async_computation.7 | async-start | bytes 2097152
  118.6 6.5 %slice-start.4 = ((s8[5242880]{0:T(1024)(128)(4,1)}), s8[4194304]{0:T(1024)(128)(4,1)S(1)}, s32[]{:S(2)}) async-start(s8[5242880]{0:T(1024)(128)(4,1)} %bitcast.117), calls=%async_computation.4 | async-start | bytes 8388608
  118.6 6.5 %slice-start.5 = ((s8[5242880]{0:T(1024)(128)(4,1)}), s8[1048576]{0:T(1024)(128)(4,1)S(1)}, s32[]{:S(2)}) async-start(s8[5242880]{0:T(1024)(128)(4,1)} %bitcast.117), calls=%async_computation.5 | async-start | bytes 2097152
  118.6 11.9 %slice-start = ((s8[5242880]{0:T(1024)(128)(4,1)}), s8[4194304]{0:T(1024)(128)(4,1)S(1)}, s32[]{:S(2)}) async-start(s8[5242880]{0:T(1024)(128)(4,1)} %bitcast.109), calls=%async_computation | async-start | bytes 8388608
  125.1 5.4 %slice-start.1 = ((s8[5242880]{0:T(1024)(128)(4,1)}), s8[1048576]{0:T(1024)(128)(4,1)S(1)}, s32[]{:S(2)}) async-start(s8[5242880]{0:T(1024)(128)(4,1)} %bitcast.109), calls=%async_computation.1 | async-start | bytes 2097152
  125.1 10.9 %slice-start.10 = ((s8[5242880]{0:T(1024)(128)(4,1)}), s8[1048576]{0:T(1024)(128)(4,1)S(1)}, s32[]{:S(2)}) async-start(s8[5242880]{0:T(1024)(128)(4,1)} %bitcast.126), calls=%async_computation.10 | async-start | bytes 2097152
  125.1 16.6 %slice-start.8 = ((s8[5242880]{0:T(1024)(128)(4,1)}), s8[4194304]{0:T(1024)(128)(4,1)S(1)}, s32[]{:S(2)}) async-start(s8[5242880]{0:T(1024)(128)(4,1)} %bitcast.124), calls=%async_computation.8 | async-start | bytes 8388608
  130.5 5.5 %slice-start.11 = ((s8[5242880]{0:T(1024)(128)(4,1)}), s8[4194304]{0:T(1024)(128)(4,1)S(1)}, s32[]{:S(2)}) async-start(s8[5242880]{0:T(1024)(128)(4,1)} %bitcast.126), calls=%async_computation.11 | async-start | bytes 8388608
  130.5 11.2 %slice-start.9 = ((s8[5242880]{0:T(1024)(128)(4,1)}), s8[1048576]{0:T(1024)(128)(4,1)S(1)}, s32[]{:S(2)}) async-start(s8[5242880]{0:T(1024)(128)(4,1)} %bitcast.124), calls=%async_computation.9 | async-start | bytes 2097152
  190.8 3.3 copy-start
  194.2 29.1 %collective-permute-start.14 = (f32[4,2,32,1024]{3,2,1,0:T(8,128)S(1)}, f32[4,2,32,1024]{3,2,1,0:T(8,128)}, u32[]{:S(2)}, u32[]{:S(2)}) collective-permute-start(f32[4,2,32,1024]{3,2,1,0:T(8,128)S(1)} %dynamic-slice_bitcast_fusion), channel_id=1, source_target_pairs={{0,112},{16,0},{32,16},{48,32},{64,48},{80,64},{96,80},{112,96},{1... | collective-permute-start | bytes 3145736 | tf_op jit(solution)/shard_map/ppermute | solution.py:46
  201.4 27.4 %collective-permute-start.4 = (f32[4,2,32,1024]{3,2,1,0:T(8,128)S(1)}, f32[4,2,32,1024]{3,2,1,0:T(8,128)S(1)}, u32[]{:S(2)}, u32[]{:S(2)}) collective-permute-start(f32[4,2,32,1024]{3,2,1,0:T(8,128)S(1)} %dynamic-slice_bitcast_fusion.1), channel_id=1, source_target_pairs={{0,16},{16,32},{32,48},{48,64},{64,80},{80,96},{96,112},{112,0},{1... | collective-permute-start | bytes 3145736 | tf_op jit(solution)/shard_map/ppermute | solution.py:45
  224.9 26.7 %collective-permute-start.15 = (f32[4,2,32,1024]{3,2,1,0:T(8,128)S(1)}, f32[4,2,32,1024]{3,2,1,0:T(8,128)}, u32[]{:S(2)}, u32[]{:S(2)}) collective-permute-start(f32[4,2,32,1024]{3,2,1,0:T(8,128)S(1)} %bitcast_add_fusion.6), channel_id=1, source_target_pairs={{0,112},{16,0},{32,16},{48,32},{64,48},{80,64},{96,80},{112,96},{1... | collective-permute-start | bytes 3145736 | tf_op jit(solution)/shard_map/ppermute | solution.py:46
  230.2 27.0 %collective-permute-start.5 = (f32[4,2,32,1024]{3,2,1,0:T(8,128)S(1)}, f32[4,2,32,1024]{3,2,1,0:T(8,128)S(1)}, u32[]{:S(2)}, u32[]{:S(2)}) collective-permute-start(f32[4,2,32,1024]{3,2,1,0:T(8,128)S(1)} %bitcast_add_fusion.13), channel_id=1, source_target_pairs={{0,16},{16,32},{32,48},{48,64},{64,80},{80,96},{96,112},{112,0},{1... | collective-permute-start | bytes 3145736 | tf_op jit(solution)/shard_map/ppermute | solution.py:45
  253.3 25.9 %collective-permute-start.16 = (f32[4,2,32,1024]{3,2,1,0:T(8,128)S(1)}, f32[4,2,32,1024]{3,2,1,0:T(8,128)}, u32[]{:S(2)}, u32[]{:S(2)}) collective-permute-start(f32[4,2,32,1024]{3,2,1,0:T(8,128)S(1)} %bitcast_add_fusion.5), channel_id=1, source_target_pairs={{0,112},{16,0},{32,16},{48,32},{64,48},{80,64},{96,80},{112,96},{1... | collective-permute-start | bytes 3145736 | tf_op jit(solution)/shard_map/ppermute | solution.py:46
  258.6 26.2 %collective-permute-start.6 = (f32[4,2,32,1024]{3,2,1,0:T(8,128)S(1)}, f32[4,2,32,1024]{3,2,1,0:T(8,128)S(1)}, u32[]{:S(2)}, u32[]{:S(2)}) collective-permute-start(f32[4,2,32,1024]{3,2,1,0:T(8,128)S(1)} %bitcast_add_fusion.12), channel_id=1, source_target_pairs={{0,16},{16,32},{32,48},{48,64},{64,80},{80,96},{96,112},{112,0},{1... | collective-permute-start | bytes 3145736 | tf_op jit(solution)/shard_map/ppermute | solution.py:45
  280.9 25.0 %collective-permute-start.17 = (f32[4,2,32,1024]{3,2,1,0:T(8,128)S(1)}, f32[4,2,32,1024]{3,2,1,0:T(8,128)}, u32[]{:S(2)}, u32[]{:S(2)}) collective-permute-start(f32[4,2,32,1024]{3,2,1,0:T(8,128)S(1)} %bitcast_add_fusion.4), channel_id=1, source_target_pairs={{0,112},{16,0},{32,16},{48,32},{64,48},{80,64},{96,80},{112,96},{1... | collective-permute-start | bytes 3145736 | tf_op jit(solution)/shard_map/ppermute | solution.py:46
  286.2 25.3 %collective-permute-start.7 = (f32[4,2,32,1024]{3,2,1,0:T(8,128)S(1)}, f32[4,2,32,1024]{3,2,1,0:T(8,128)S(1)}, u32[]{:S(2)}, u32[]{:S(2)}) collective-permute-start(f32[4,2,32,1024]{3,2,1,0:T(8,128)S(1)} %bitcast_add_fusion.11), channel_id=1, source_target_pairs={{0,16},{16,32},{32,48},{48,64},{64,80},{80,96},{96,112},{112,0},{1... | collective-permute-start | bytes 3145736 | tf_op jit(solution)/shard_map/ppermute | solution.py:45
  307.6 24.1 %collective-permute-start.18 = (f32[4,2,32,1024]{3,2,1,0:T(8,128)S(1)}, f32[4,2,32,1024]{3,2,1,0:T(8,128)}, u32[]{:S(2)}, u32[]{:S(2)}) collective-permute-start(f32[4,2,32,1024]{3,2,1,0:T(8,128)S(1)} %bitcast_add_fusion.3), channel_id=1, source_target_pairs={{0,112},{16,0},{32,16},{48,32},{64,48},{80,64},{96,80},{112,96},{1... | collective-permute-start | bytes 3145736 | tf_op jit(solution)/shard_map/ppermute | solution.py:46
  312.8 24.4 %collective-permute-start.8 = (f32[4,2,32,1024]{3,2,1,0:T(8,128)S(1)}, f32[4,2,32,1024]{3,2,1,0:T(8,128)S(1)}, u32[]{:S(2)}, u32[]{:S(2)}) collective-permute-start(f32[4,2,32,1024]{3,2,1,0:T(8,128)S(1)} %bitcast_add_fusion.10), channel_id=1, source_target_pairs={{0,16},{16,32},{32,48},{48,64},{64,80},{80,96},{96,112},{112,0},{1... | collective-permute-start | bytes 3145736 | tf_op jit(solution)/shard_map/ppermute | solution.py:45
  333.3 23.1 %collective-permute-start.19 = (f32[4,2,32,1024]{3,2,1,0:T(8,128)S(1)}, f32[4,2,32,1024]{3,2,1,0:T(8,128)}, u32[]{:S(2)}, u32[]{:S(2)}) collective-permute-start(f32[4,2,32,1024]{3,2,1,0:T(8,128)S(1)} %bitcast_add_fusion.2), channel_id=1, source_target_pairs={{0,112},{16,0},{32,16},{48,32},{64,48},{80,64},{96,80},{112,96},{1... | collective-permute-start | bytes 3145736 | tf_op jit(solution)/shard_map/ppermute | solution.py:46
  339.5 23.0 %collective-permute-start.9 = (f32[4,2,32,1024]{3,2,1,0:T(8,128)}, f32[4,2,32,1024]{3,2,1,0:T(8,128)}, u32[]{:S(2)}, u32[]{:S(2)}) collective-permute-start(f32[4,2,32,1024]{3,2,1,0:T(8,128)} %bitcast_add_fusion.9), channel_id=1, source_target_pairs={{0,16},{16,32},{32,48},{48,64},{64,80},{80,96},{96,112},{112,0},{1... | collective-permute-start | bytes 3145736 | tf_op jit(solution)/shard_map/ppermute | solution.py:45
  358.2 22.2 %collective-permute-start.20 = (f32[4,2,32,1024]{3,2,1,0:T(8,128)S(1)}, f32[4,2,32,1024]{3,2,1,0:T(8,128)S(1)}, u32[]{:S(2)}, u32[]{:S(2)}) collective-permute-start(f32[4,2,32,1024]{3,2,1,0:T(8,128)S(1)} %bitcast_add_fusion.1), channel_id=1, source_target_pairs={{0,112},{16,0},{32,16},{48,32},{64,48},{80,64},{96,80},{112,96},{1... | collective-permute-start | bytes 3145736 | tf_op jit(solution)/shard_map/ppermute | solution.py:46
  364.2 21.9 %collective-permute-start.10 = (f32[4,2,32,1024]{3,2,1,0:T(8,128)S(1)}, f32[4,2,32,1024]{3,2,1,0:T(8,128)}, u32[]{:S(2)}, u32[]{:S(2)}) collective-permute-start(f32[4,2,32,1024]{3,2,1,0:T(8,128)S(1)} %bitcast_add_fusion.8), channel_id=1, source_target_pairs={{0,16},{16,32},{32,48},{48,64},{64,80},{80,96},{96,112},{112,0},{1... | collective-permute-start | bytes 3145736 | tf_op jit(solution)/shard_map/ppermute | solution.py:45
  381.8 8.6 %collective-permute-start.21 = (f32[2,32,1024]{2,1,0:T(8,128)S(1)}, f32[2,32,1024]{2,1,0:T(8,128)}, u32[]{:S(2)}, u32[]{:S(2)}) collective-permute-start(f32[2,32,1024]{2,1,0:T(8,128)S(1)} %dynamic-slice_bitcast_fusion.2), channel_id=1, source_target_pairs={{0,12},{4,0},{8,4},{12,8},{1,13},{5,1},{9,5},{13,9},{2,14},{6,2},{... | collective-permute-start | bytes 786440 | tf_op jit(solution)/shard_map/ppermute | solution.py:46
  387.9 10.2 %collective-permute-start.11 = (f32[2,32,1024]{2,1,0:T(8,128)S(1)}, f32[2,32,1024]{2,1,0:T(8,128)S(1)}, u32[]{:S(2)}, u32[]{:S(2)}) collective-permute-start(f32[2,32,1024]{2,1,0:T(8,128)S(1)} %dynamic-slice_bitcast_fusion.3), channel_id=1, source_target_pairs={{0,4},{4,8},{8,12},{12,0},{1,5},{5,9},{9,13},{13,1},{2,6},{6,10},{... | collective-permute-start | bytes 786440 | tf_op jit(solution)/shard_map/ppermute | solution.py:45
  391.4 7.8 %collective-permute-start.22 = (f32[2,32,1024]{2,1,0:T(8,128)S(1)}, f32[2,32,1024]{2,1,0:T(8,128)S(1)}, u32[]{:S(2)}, u32[]{:S(2)}) collective-permute-start(f32[2,32,1024]{2,1,0:T(8,128)S(1)} %bitcast_add_fusion.16), channel_id=1, source_target_pairs={{0,12},{4,0},{8,4},{12,8},{1,13},{5,1},{9,5},{13,9},{2,14},{6,2},{... | collective-permute-start | bytes 786440 | tf_op jit(solution)/shard_map/ppermute | solution.py:46
  398.1 9.6 %collective-permute-start.12 = (f32[2,32,1024]{2,1,0:T(8,128)S(1)}, f32[2,32,1024]{2,1,0:T(8,128)S(1)}, u32[]{:S(2)}, u32[]{:S(2)}) collective-permute-start(f32[2,32,1024]{2,1,0:T(8,128)S(1)} %bitcast_add_fusion.19), channel_id=1, source_target_pairs={{0,4},{4,8},{8,12},{12,0},{1,5},{5,9},{9,13},{13,1},{2,6},{6,10},{... | collective-permute-start | bytes 786440 | tf_op jit(solution)/shard_map/ppermute | solution.py:45
  399.2 8.6 %collective-permute-start.23 = (f32[2,32,1024]{2,1,0:T(8,128)S(1)}, f32[2,32,1024]{2,1,0:T(8,128)S(1)}, u32[]{:S(2)}, u32[]{:S(2)}) collective-permute-start(f32[2,32,1024]{2,1,0:T(8,128)S(1)} %bitcast_add_fusion.15), channel_id=1, source_target_pairs={{0,12},{4,0},{8,4},{12,8},{1,13},{5,1},{9,5},{13,9},{2,14},{6,2},{... | collective-permute-start | bytes 786440 | tf_op jit(solution)/shard_map/ppermute | solution.py:46
  407.7 7.7 %collective-permute-start.13 = (f32[2,32,1024]{2,1,0:T(8,128)S(1)}, f32[2,32,1024]{2,1,0:T(8,128)S(1)}, u32[]{:S(2)}, u32[]{:S(2)}) collective-permute-start(f32[2,32,1024]{2,1,0:T(8,128)S(1)} %bitcast_add_fusion.18), channel_id=1, source_target_pairs={{0,4},{4,8},{8,12},{12,0},{1,5},{5,9},{9,13},{13,1},{2,6},{6,10},{... | collective-permute-start | bytes 786440 | tf_op jit(solution)/shard_map/ppermute | solution.py:45
  415.4 6.8 %collective-permute-start.24 = (f32[32,2048]{1,0:T(8,128)S(1)}, f32[32,2048]{1,0:T(8,128)S(1)}, u32[]{:S(2)}, u32[]{:S(2)}) collective-permute-start(f32[32,2048]{1,0:T(8,128)S(1)} %fusion.42), channel_id=1, source_target_pairs={{0,2},{2,0},{1,3},{3,1},{4,6},{6,4},{5,7},{7,5},{8,10},{10,8},{9,1... | collective-permute-start | bytes 786440 | tf_op jit(solution)/shard_map/ppermute | solution.py:36
